TPU v7x, 32 devices: a whole 2x2x4 slice. The times are simulated.
32 devices in a mesh: rows: 32 (over z, y, x, core).
Axes of the slice: x: 2, y: 2, z: 4, core: 2. Of those that a mesh axis runs over, the one named last changes fastest.
Arguments:
- inputs: bfloat16 [32768, 768], P('rows'), may hold values from -6 to 6
- context_count: int32 [32], P('rows'), may hold values from 64 to 768, as said below
- query_count: int32 [32], P('rows'), may hold values from 1 to 256, as said below
- row_mask: int32 [32768], P('rows'), may hold values 0 or 1
- ln1_gain: float32 [768], replicated, may hold values from 0.25 to 1.75
- ln1_bias: float32 [768], replicated, may hold values from -3 to 3
- w_qkv: bfloat16 [768, 2304], replicated, may hold values from -0.21875 to 0.21875
- w_out: bfloat16 [768, 768], replicated, may hold values from -2 to 2
- ln2_gain: float32 [768], replicated, may hold values from 0.25 to 1.75
- ln2_bias: float32 [768], replicated, may hold values from -3 to 3
- w_up: bfloat16 [768, 3072], replicated, may hold values from -0.21875 to 0.21875
- w_down: bfloat16 [3072, 768], replicated, may hold values from -0.109375 to 0.109375
- cotangent: bfloat16 [32768, 768], P('rows'), may hold values from -6 to 6
Outputs:
- layer_out: bfloat16 [32768, 768], P('rows')
- grad_inputs: float32 [32768, 768], P('rows')
- grad_ln1_gain: float32 [768], replicated
- grad_ln1_bias: float32 [768], replicated
- grad_qkv: float32 [768, 2304], replicated
- grad_out: float32 [768, 768], replicated
- grad_ln2_gain: float32 [768], replicated
- grad_ln2_bias: float32 [768], replicated
- grad_up: float32 [768, 3072], P(None, 'rows')
- grad_down: float32 [3072, 768], P('rows')
Inputs may be any that keep to these rules, and one draw needn't show every extreme that they name: `context_count`: context rows of each table; in every draw some table has exactly 768 and some exactly 64. `query_count`: query rows of each table; in every draw some table has exactly 256.
All inputs are finite; a program needn't handle non-finite values. No bound on the sum of `row_mask` on one device may be relied on, other than what follows from the above.
Results may differ from a plain program's by a relative error of at most 0.0096.
Values sent between devices are 32-bit elements; how exact they have to be, the bound alone decides.
No kernel may reach another device: no remote copies, remote signals or barrier semaphores. Data moves between devices by JAX's collectives and lax.ppermute only.
A program may use at most 256 MiB of HBM per device.

v0:
```python
from functools import partial
import math

import jax
import jax.numpy as jnp
from jax import lax
from jax.sharding import PartitionSpec as P

HEADS = 12
HEAD = 64


epsilon = 1e-05
masked_score = -1000000000.0


def normalize(values, norm_gain, norm_bias):
    centre = jnp.mean(values, axis=-1, keepdims=True)
    centred = values - centre
    spread = jnp.mean(centred * centred, axis=-1, keepdims=True)
    inverse = lax.rsqrt(spread + epsilon)
    unit_rows = centred * inverse
    return (unit_rows * norm_gain + norm_bias, unit_rows, inverse)


def norm_back(grad_norm, unit_rows, inverse, norm_gain):
    grad_unit = grad_norm * norm_gain
    grad_mean = jnp.mean(grad_unit, axis=-1, keepdims=True)
    grad_proj = jnp.mean(grad_unit * unit_rows, axis=-1, keepdims=True)
    grad_values = inverse * (grad_unit - grad_mean - unit_rows * grad_proj)
    return (grad_values, jnp.sum(grad_norm * unit_rows, axis=0), jnp.sum(grad_norm, axis=0))


def contract_rows(left, right):
    return lax.dot_general(
        left, right, (((0,), (0,)), ((), ())), preferred_element_type=jnp.float32
    )


def contract_cols(left, right):
    return lax.dot_general(
        left, right, (((1,), (1,)), ((), ())), preferred_element_type=jnp.float32
    )


def score_block(query_block, key_rows, key_live):
    score_factor = 1.0 / math.sqrt(query_block.shape[2])
    scores = (
        jnp.einsum("qhe,khe->hqk", query_block, key_rows, preferred_element_type=jnp.float32)
        * score_factor
    )
    return jnp.where(key_live[None, None, :], scores, masked_score)


def split_packed(packed, keys_len):
    slots, triple = packed.shape
    width = triple // 3
    query_rows = packed[:, :width].reshape(slots, HEADS, HEAD)
    key_rows = packed[:keys_len, width : 2 * width].reshape(keys_len, HEADS, HEAD)
    value_rows = packed[:keys_len, 2 * width :].reshape(keys_len, HEADS, HEAD)
    return (query_rows, key_rows, value_rows)


def forward_pass(inputs, row_live, key_live, params):
    ln1_gain, ln1_bias, w_qkv, w_out, ln2_gain, ln2_bias, w_up, w_down = params
    slots, width = inputs.shape
    keys_len = key_live.shape[0]
    block_len = min(512, slots)
    rows_wide = inputs.astype(jnp.float32)
    normed, unit_one, inverse_one = normalize(rows_wide, ln1_gain, ln1_bias)
    normed_low = normed.astype(jnp.bfloat16)
    packed = jnp.dot(normed_low, w_qkv, preferred_element_type=jnp.float32).astype(jnp.bfloat16)
    query_rows, key_rows, value_rows = split_packed(packed, keys_len)
    attended_parts = []
    norm_parts = []
    for first_row in range(0, slots, block_len):
        scores = score_block(query_rows[first_row : first_row + block_len], key_rows, key_live)
        row_max = jnp.max(scores, axis=-1, keepdims=True)
        exponent = jnp.exp(scores - row_max)
        row_total = jnp.sum(exponent, axis=-1, keepdims=True)
        attn_probs = (exponent / row_total).astype(jnp.bfloat16)
        attended_parts.append(
            jnp.einsum("hqk,khe->qhe", attn_probs, value_rows, preferred_element_type=jnp.float32)
        )
        norm_parts.append(row_max + jnp.log(row_total))
    attended = jnp.concatenate(attended_parts, axis=0).reshape(slots, width)
    attended_low = jnp.where(row_live[:, None], attended, 0.0).astype(jnp.bfloat16)
    log_norm = jnp.concatenate(norm_parts, axis=1)
    hidden_rows = rows_wide + jnp.dot(attended_low, w_out, preferred_element_type=jnp.float32)
    normed_two, unit_two, inverse_two = normalize(hidden_rows, ln2_gain, ln2_bias)
    normed_two_low = normed_two.astype(jnp.bfloat16)
    pre_act = jnp.dot(normed_two_low, w_up, preferred_element_type=jnp.float32)
    activated_low = jax.nn.gelu(pre_act, approximate=False).astype(jnp.bfloat16)
    layer_out = hidden_rows + jnp.dot(activated_low, w_down, preferred_element_type=jnp.float32)
    stash = (
        normed_low,
        unit_one,
        inverse_one,
        packed,
        attended_low,
        log_norm,
        unit_two,
        inverse_two,
        normed_two_low,
        pre_act,
        activated_low,
    )
    return (layer_out, stash)


def local(
    inputs,
    context_count,
    query_count,
    row_mask,
    ln1_gain,
    ln1_bias,
    w_qkv,
    w_out,
    ln2_gain,
    ln2_bias,
    w_up,
    w_down,
    cotangent,
):
    slots, width = inputs.shape
    keys_len = slots * 3 // 4
    block_len = min(512, slots)
    query_sum = lax.psum(query_count[0].astype(jnp.float32), "rows")
    loss_factor = math.sqrt(lax.axis_size("rows")) * (slots // 4) / query_sum
    positions = jnp.arange(slots, dtype=jnp.int32)
    present = (row_mask == 1) | (positions == 0)
    context = context_count[0]
    row_live = present & (positions < context + query_count[0])
    key_live = (present & (positions < context))[:keys_len]
    is_query = row_live & (positions >= context)
    params = (ln1_gain, ln1_bias, w_qkv, w_out, ln2_gain, ln2_bias, w_up, w_down)
    layer_out, stash = forward_pass(inputs, row_live, key_live, params)
    inputs_again, finished = lax.optimization_barrier((inputs, layer_out))
    stash = forward_pass(inputs_again, row_live, key_live, params)[1]
    (
        normed_low,
        unit_one,
        inverse_one,
        packed,
        attended_low,
        log_norm,
        unit_two,
        inverse_two,
        normed_two_low,
        pre_act,
        activated_low,
    ) = stash
    upstream = cotangent.astype(jnp.float32) * jnp.where(is_query[:, None], loss_factor, 0.0)
    upstream_low = upstream.astype(jnp.bfloat16)
    grad_down = contract_rows(activated_low, upstream_low)
    grad_act = contract_cols(upstream_low, w_down)
    grad_pre = jax.vjp(partial(jax.nn.gelu, approximate=False), pre_act)[1](grad_act)[0]
    grad_pre_low = grad_pre.astype(jnp.bfloat16)
    grad_up_cols = contract_rows(grad_pre_low, normed_two_low)
    down_share, up_share = (
        lax.psum_scatter(grad_down, "rows", scatter_dimension=0, tiled=True),
        lax.psum_scatter(grad_up_cols, "rows", scatter_dimension=0, tiled=True),
    )
    grad_normed_two = contract_cols(grad_pre_low, w_up)
    grad_hidden_norm, grad_gain_two, grad_bias_two = norm_back(
        grad_normed_two, unit_two, inverse_two, ln2_gain
    )
    grad_hidden = upstream + grad_hidden_norm
    grad_hidden_low = grad_hidden.astype(jnp.bfloat16)
    grad_wout = contract_rows(attended_low, grad_hidden_low)
    grad_attended = contract_cols(grad_hidden_low, w_out)
    grad_attended = (
        jnp.where(row_live[:, None], grad_attended, 0.0)
        .astype(jnp.bfloat16)
        .reshape(slots, HEADS, HEAD)
    )
    query_rows, key_rows, value_rows = split_packed(packed, keys_len)
    score_factor = 1.0 / math.sqrt(HEAD)
    grad_keys = jnp.zeros((keys_len, HEADS, HEAD), jnp.float32)
    grad_values = jnp.zeros((keys_len, HEADS, HEAD), jnp.float32)
    grad_query_parts = []
    for first_row in range(0, slots, block_len):
        query_block = query_rows[first_row : first_row + block_len]
        grad_block = grad_attended[first_row : first_row + block_len]
        scores = score_block(query_block, key_rows, key_live)
        attn_probs = jnp.exp(scores - log_norm[:, first_row : first_row + block_len])
        probs_low = attn_probs.astype(jnp.bfloat16)
        grad_values = grad_values + jnp.einsum(
            "hqk,qhe->khe", probs_low, grad_block, preferred_element_type=jnp.float32
        )
        grad_probs = jnp.einsum(
            "qhe,khe->hqk", grad_block, value_rows, preferred_element_type=jnp.float32
        )
        inner = jnp.sum(grad_probs * attn_probs, axis=-1, keepdims=True)
        grad_scores = (attn_probs * (grad_probs - inner)).astype(jnp.bfloat16)
        grad_query_parts.append(
            jnp.einsum("hqk,khe->qhe", grad_scores, key_rows, preferred_element_type=jnp.float32)
            * score_factor
        )
        grad_keys = (
            grad_keys
            + jnp.einsum(
                "hqk,qhe->khe", grad_scores, query_block, preferred_element_type=jnp.float32
            )
            * score_factor
        )
    pad_rows = slots - keys_len
    grad_packed = jnp.concatenate(
        [
            jnp.concatenate(grad_query_parts, axis=0).reshape(slots, width),
            jnp.pad(grad_keys.reshape(keys_len, width), ((0, pad_rows), (0, 0))),
            jnp.pad(grad_values.reshape(keys_len, width), ((0, pad_rows), (0, 0))),
        ],
        axis=1,
    ).astype(jnp.bfloat16)
    grad_qkv_local = contract_rows(normed_low, grad_packed)
    grad_normed = contract_cols(grad_packed, w_qkv)
    grad_rows_norm, grad_gain_one, grad_bias_one = norm_back(
        grad_normed, unit_one, inverse_one, ln1_gain
    )
    grad_inputs = grad_hidden + grad_rows_norm
    summed = lax.psum(
        (grad_gain_one, grad_bias_one, grad_qkv_local, grad_wout, grad_gain_two, grad_bias_two),
        "rows",
    )
    return (
        layer_out.astype(jnp.bfloat16),
        grad_inputs,
        summed[0],
        summed[1],
        summed[2],
        summed[3],
        summed[4],
        summed[5],
        up_share.T,
        down_share,
    )


def solution(mesh):
    placed = (
        P("rows", None),
        P("rows"),
        P("rows"),
        P("rows"),
        P(),
        P(),
        P(),
        P(),
        P(),
        P(),
        P(),
        P(),
        P("rows", None),
    )
    return jax.shard_map(
        local,
        mesh=mesh,
        in_specs=placed,
        out_specs=(
            P("rows", None),
            P("rows", None),
            P(),
            P(),
            P(),
            P(),
            P(),
            P(),
            P(None, "rows"),
            P("rows", None),
        ),
        check_vma=False,
    )
```

profile of v0, /device:TPU:0, one launch (start us, length us, event | category | flops | bytes accessed | tf_op | source)
XLA Modules:
  0.0 916.2 jit_solution(1645850470950216768)
XLA Ops:
  13.6 6.3 convolution_convert_fusion.1
  28.7 42.2 %psum.49 = f32[]{:T(128)} all-reduce(f32[]{:T(128)S(6)} %convert_element_type.95), channel_id=1, replica_groups=mesh['rows'=32] {'rows'}, use_global_device_ids=true, to_apply=%region_8.9 | all-reduce | flops 1 | bytes 8 | tf_op jit(solution)/shard_map/psum | solution.py:129
  76.8 11.8 %fusion.158 = (f32[12,512]{1,0:T(8,128)}, f32[12,512,768]{2,1,0:T(8,128)}) fusion(pred[768]{0:T(1024)(128)(4,1)S(1)} %bitcast.131, bf16[512,12,64]{0,2,1:T(8,128)(2,1)} %bitcast.129, bf16[768,12,64]{0,2,1:T(8,128)(2,1)} %bitcast.125), kind=kOutput, calls=%fused_computation.228 | convolution fusion | flops 622854912 | bytes 20865792 | tf_op jit(solution)/shard_map/sub | solution.py:79
  88.6 11.8 %fusion.157 = (f32[12,512]{1,0:T(8,128)}, f32[12,512,768]{2,1,0:T(8,128)}) fusion(pred[768]{0:T(1024)(128)(4,1)S(1)} %bitcast.132, bf16[512,12,64]{0,2,1:T(8,128)(2,1)} %bitcast.130, bf16[768,12,64]{0,2,1:T(8,128)(2,1)} %bitcast.126), kind=kOutput, calls=%fused_computation.227 | convolution fusion | flops 622854912 | bytes 20865792 | tf_op jit(solution)/shard_map/sub | solution.py:79
  100.4 8.5 fusion.90
  108.9 8.0 fusion.89
  120.7 32.6 %fusion.222 = bf16[1024,3072]{1,0:T(8,128)(2,1)S(1)} fusion(bf16[768,3072]{1,0:T(8,128)(2,1)S(1)} %bitcast.138, f32[1024,768]{0,1:T(8,128)S(1)} %get-tuple-element.62, f32[768]{0:T(1024)S(1)} %copy-done.58, f32[768]{0:T(1024)S(1)} %copy-done.42, f32[1024]{0:T(1024)S(1)} %add_rsqrt_fusion.2, f32[1024]{0:T(1024)S(1)} %broadcast_multiply_fusion.6), kind=kOutput, calls=%fused_computation.32.clone.clone.clone.clone.1 | convolution fusion | flops 5040242688 | bytes 14170112 | tf_op jit(solution)/shard_map/dot_general | solution.py:92
  153.4 6.3 fusion.72
  165.9 6.3 convolution_convert_fusion
  193.8 9.8 %fusion.88 = bf16[512,12,64]{0,2,1:T(8,128)(2,1)} fusion(bf16[768,12,64]{0,2,1:T(8,128)(2,1)S(1)} %bitcast.107, f32[12,512,768]{2,1,0:T(8,128)} %copy-done.1, f32[12,512]{1,0:T(8,128)S(1)} %fusion.2, f32[12,512]{1,0:T(8,128)S(1)} %get-tuple-element.65), kind=kOutput, calls=%fused_computation.150 | convolution fusion | flops 618135552 | bytes 20889600 | tf_op jit(solution)/shard_map/hqk,khe->qhe/dot_general | solution.py:83
  210.5 6.5 copy-done.2
  220.9 8.8 fusion.87
  234.4 36.0 %fusion.11 = (f32[1024,3072]{1,0:T(8,128)}, f32[1024,3072]{1,0:T(8,128)}) fusion(bf16[768,3072]{1,0:T(8,128)(2,1)S(1)} %bitcast.140, f32[1024,768]{0,1:T(8,128)S(1)} %get-tuple-element.68, f32[1024]{0:T(1024)S(1)} %add_rsqrt_fusion, f32[1024]{0:T(1024)S(1)} %broadcast_multiply_fusion.4, f32[768]{0:T(1024)S(1)} %copy-done.59, f32[768]{0:T(1024)S(1)} %copy-done.42), kind=kOutput, calls=%fused_computation.33 | convolution fusion | flops 5030805504 | bytes 33044480 | tf_op jit(solution)/shard_map/dot_general | solution.py:92
  273.0 18.3 %add_convert_fusion = bf16[1024,3072]{1,0:T(8,128)(2,1)} fusion(f32[1024,3072]{1,0:T(8,128)} %get-tuple-element.69, f32[1024,3072]{1,0:T(8,128)} %get-tuple-element.70, bf16[3072,768]{1,0:T(8,128)(2,1)} %param.24, bf16[1024,768]{0,1:T(8,128)(2,1)} %copy.57, f32[1024]{0:T(1024)S(1)} %copy-done.35), kind=kOutput, calls=%fused_computation.35 | convolution fusion | flops 4878237696 | bytes 37752832 | tf_op jit(solution)/shard_map/dot_general | solution.py:41
  291.3 10.3 %fusion.164 = (f32[768]{0:T(1024)}, f32[1024,768]{1,0:T(8,128)}) fusion(bf16[1024,3072]{1,0:T(8,128)(2,1)} %add_convert_fusion, bf16[768,3072]{1,0:T(8,128)(2,1)} %param.23), kind=kOutput, calls=%fused_computation.234 | convolution fusion | flops 4832623616 | bytes 14158848 | tf_op jit(solution)/shard_map/dot_general | solution.py:41
  305.2 4.6 multiply_reduce_fusion.2
  317.2 16.2 %multiply_reduce_fusion.1 = (f32[12,512]{1,0:T(8,128)S(1)}, f32[12,512,768]{2,1,0:T(8,128)}) fusion(f32[12,512,768]{2,1,0:T(8,128)} %copy-done.1, f32[12,512]{1,0:T(8,128)S(1)} %copy-done.26, bf16[512,12,64]{0,2,1:T(8,128)(2,1)S(1)} %bitcast.115, bf16[768,12,64]{0,2,1:T(8,128)(2,1)S(1)} %bitcast.109), kind=kOutput, calls=%fused_computation.8 | convolution fusion | flops 618129408 | bytes 39763968 | tf_op jit(solution)/shard_map/qhe,khe->hqk/dot_general | solution.py:192
  333.4 13.0 %multiply_convert_fusion.1 = bf16[12,512,768]{2,1,0:T(8,128)(2,1)S(1)} fusion(f32[12,512,768]{2,1,0:T(8,128)} %get-tuple-element.72, f32[12,512,768]{2,1,0:T(8,128)} %copy-done.1, f32[12,512]{1,0:T(8,128)S(1)} %get-tuple-element.71, f32[12,512]{1,0:T(8,128)S(1)} %copy-done.26), kind=kLoop, calls=%fused_computation.7 | loop fusion | flops 18874368 | bytes 47235072 | tf_op jit(solution)/shard_map/convert_element_type | solution.py:196
  353.5 16.0 %multiply_reduce_fusion = (f32[12,512]{1,0:T(8,128)S(1)}, f32[12,512,768]{2,1,0:T(8,128)}) fusion(f32[12,512,768]{2,1,0:T(8,128)} %copy-done.2, f32[12,512]{1,0:T(8,128)S(1)} %log_add_fusion, bf16[512,12,64]{0,2,1:T(8,128)(2,1)S(1)} %bitcast.117, bf16[768,12,64]{0,2,1:T(8,128)(2,1)S(1)} %bitcast.110), kind=kOutput, calls=%fused_computation.5 | convolution fusion | flops 618129408 | bytes 39763968 | tf_op jit(solution)/shard_map/qhe,khe->hqk/dot_general | solution.py:192
  369.4 9.5 %fusion.24 = f32[12,64,768]{2,1,0:T(8,128)} fusion(bf16[512,12,64]{0,2,1:T(8,128)(2,1)S(1)} %bitcast.118, f32[12,512,768]{2,1,0:T(8,128)} %copy-done.2, f32[12,512]{1,0:T(8,128)S(1)} %log_add_fusion), kind=kOutput, calls=%fused_computation.64 | convolution fusion | flops 613416960 | bytes 22044672 | tf_op jit(solution)/shard_map/hqk,qhe->khe/dot_general | solution.py:189
  378.9 12.9 %multiply_convert_fusion = bf16[12,512,768]{2,1,0:T(8,128)(2,1)S(1)} fusion(f32[12,512,768]{2,1,0:T(8,128)} %get-tuple-element.74, f32[12,512,768]{2,1,0:T(8,128)} %copy-done.2, f32[12,512]{1,0:T(8,128)S(1)} %get-tuple-element.73, f32[12,512]{1,0:T(8,128)S(1)} %log_add_fusion), kind=kLoop, calls=%fused_computation.4 | loop fusion | flops 18874368 | bytes 47235072 | tf_op jit(solution)/shard_map/convert_element_type | solution.py:196
  399.3 7.3 multiply_convert_fusion.4
  407.2 6.2 add_convert_fusion.3
  416.1 8.7 fusion.142
  424.9 16.5 %fusion.43 = f32[3072,768]{1,0:T(8,128)} fusion(f32[1024,3072]{1,0:T(8,128)} %get-tuple-element.69, f32[1024,3072]{1,0:T(8,128)} %get-tuple-element.70, bf16[1024,768]{0,1:T(8,128)(2,1)} %copy.57, f32[1024]{0:T(1024)S(1)} %copy-done.35), kind=kOutput, calls=%fused_computation.82 | convolution fusion | flops 4843634688 | bytes 36179968 | tf_op jit(solution)/shard_map/dot_general | solution.py:35
  442.1 11.2 %fusion.148 = f32[3072,768]{1,0:T(8,128)} fusion(bf16[1024,3072]{1,0:T(8,128)(2,1)} %add_convert_fusion, f32[1024,768]{0,1:T(8,128)} %copy-done.8, f32[1024]{0:T(1024)S(1)} %copy-done.37, f32[1024]{0:T(1024)S(1)} %broadcast_multiply_fusion.4, f32[768]{0:T(1024)} %param.22, f32[768]{0:T(1024)} %param.21), kind=kOutput, calls=%fused_computation.220 | convolution fusion | flops 4835770368 | bytes 18888704 | tf_op jit(solution)/shard_map/dot_general | solution.py:35
  455.9 8.3 fusion.163
  480.1 41.1 %all-reduce.2 = (f32[768]{0:T(1024)}, f32[768]{0:T(1024)}, f32[768]{0:T(1024)}, f32[768]{0:T(1024)}) all-reduce(f32[768]{0:T(1024)S(1)} %get-tuple-element.34, f32[768]{0:T(1024)S(1)} %copy-done.51, f32[768]{0:T(1024)S(1)} %copy-done.43, f32[768]{0:T(1024)S(1)} %copy-done.50), channel_id=1, replica_groups=mesh['rows'=32] {'rows'}, use_global_device_ids=true, to_apply=%region_24.25 | all-reduce | flops 3072 | bytes 24576 | tf_op jit(solution)/shard_map/psum | solution.py:223
  521.2 95.8 %all-reduce.6.cloned.1.call-done = (f32[768,2304]{1,0:T(8,128)}, f32[768,768]{1,0:T(8,128)}) async-done(((f32[768,2304]{1,0:T(8,128)}, f32[768,768]{1,0:T(8,128)}), (f32[768,2304]{1,0:T(8,128)}, f32[768,768]{1,0:T(8,128)})) %all-reduce.6.cloned.1.call-update) | async-done | bytes 9437200 | tf_op jit(solution)/shard_map/psum | solution.py:223
  617.0 142.8 %reduce-scatter.5.cloned.1.call-done = f32[96,768]{1,0:T(8,128)} async-done(((f32[3072,768]{1,0:T(8,128)}), f32[96,768]{1,0:T(8,128)}) %reduce-scatter.5.cloned.1.call-update) | async-done | bytes 294928 | tf_op jit(solution)/shard_map/reduce_scatter | solution.py:162
  759.7 141.7 %reduce-scatter.3.cloned.1.call-done = f32[96,768]{1,0:T(8,128)} async-done(((f32[3072,768]{1,0:T(8,128)}), f32[96,768]{1,0:T(8,128)}) %reduce-scatter.3.cloned.1.call-update) | async-done | bytes 294928 | tf_op jit(solution)/shard_map/reduce_scatter | solution.py:163
  901.4 6.6 copy.74
  (214 shorter events, 117.8 us)
Async XLA Ops:
  7.2 609.8 %all-reduce.6.cloned.1.call-start = ((), (), s32[]{:S(2)}) async-start(), calls=%async_computation.4 | async-start | bytes 18874368 | tf_op jit(solution)/shard_map/psum | solution.py:223
  22.7 53.5 %copy-start.49 = (s32[1024]{0:T(1024)S(1)}, s32[1024]{0:T(1024)}, u32[]{:S(2)}) copy-start(s32[1024]{0:T(1024)} %param.16) | copy-start | bytes 12292
  76.8 40.4 %copy-start.44 = (pred[1024]{0:T(1024)(128)(4,1)}, pred[1024]{0:T(1024)(128)(4,1)S(1)}, u32[]{:S(2)}) copy-start(pred[1024]{0:T(1024)(128)(4,1)S(1)} %get-tuple-element.45) | copy-start | bytes 3076
  76.8 11.8 %copy-start.47 = (pred[1024]{0:T(1024)(128)(4,1)}, pred[1024]{0:T(1024)(128)(4,1)S(1)}, u32[]{:S(2)}) copy-start(pred[1024]{0:T(1024)(128)(4,1)S(1)} %fusion.100) | copy-start | bytes 3076
  100.4 8.5 copy-start.24
  100.4 8.5 copy-start.60
  118.7 34.6 %slice-start.5 = ((s8[4718592]{0:T(1024)(128)(4,1)}), s8[4194304]{0:T(1024)(128)(4,1)S(1)}, s32[]{:S(2)}) async-start(s8[4718592]{0:T(1024)(128)(4,1)} %bitcast.135), calls=%async_computation.10 | async-start | bytes 8388608
  120.7 32.6 %slice-start.6 = ((s8[4718592]{0:T(1024)(128)(4,1)}), s8[524288]{0:T(1024)(128)(4,1)S(1)}, s32[]{:S(2)}) async-start(s8[4718592]{0:T(1024)(128)(4,1)} %bitcast.135), calls=%async_computation.11 | async-start | bytes 1048576
  163.9 8.2 copy-start.31
  173.7 8.3 copy-start.48
  186.6 7.3 copy-start.14
  210.5 10.3 %copy-start.27 = (f32[12,512]{1,0:T(8,128)}, f32[12,512]{1,0:T(8,128)S(1)}, u32[]{:S(2)}) copy-start(f32[12,512]{1,0:T(8,128)S(1)} %get-tuple-element.63) | copy-start | bytes 73732
  220.8 8.9 copy-start.29
  220.9 8.9 copy-start.25
  220.9 9.1 copy-start.45
  220.9 9.6 %copy-start.53 = (bf16[768,768]{1,0:T(8,128)(2,1)S(1)}, bf16[768,768]{1,0:T(8,128)(2,1)}, u32[]{:S(2)}) copy-start(bf16[768,768]{1,0:T(8,128)(2,1)} %param.20) | copy-start | bytes 3538948
  234.3 75.5 %copy-start.36 = (f32[1024]{0:T(1024)}, f32[1024]{0:T(1024)S(1)}, u32[]{:S(2)}) copy-start(f32[1024]{0:T(1024)S(1)} %add_rsqrt_fusion) | copy-start | bytes 12292
  234.3 38.6 %copy-start.35 = (f32[1024]{0:T(1024)S(1)}, f32[1024]{0:T(1024)}, u32[]{:S(2)}) copy-start(f32[1024]{0:T(1024)} %get-tuple-element.44) | copy-start | bytes 12292
  317.2 16.3 %copy-start.19 = (bf16[512,768]{0,1:T(8,128)(2,1)}, bf16[512,768]{0,1:T(8,128)(2,1)S(1)}, u32[]{:S(2)}) copy-start(bf16[512,768]{0,1:T(8,128)(2,1)S(1)} %get-tuple-element.55) | copy-start | bytes 2359300
  333.4 13.0 %copy-start.7 = (bf16[768,768]{0,1:T(8,128)(2,1)S(1)}, bf16[768,768]{0,1:T(8,128)(2,1)}, u32[]{:S(2)}) copy-start(bf16[768,768]{0,1:T(8,128)(2,1)} %copy.61) | copy-start | bytes 3538948
  395.5 11.1 %slice-start = ((s8[18874368]{0:T(1024)(128)(4,1)}), s8[4194304]{0:T(1024)(128)(4,1)S(1)}, s32[]{:S(2)}) async-start(s8[18874368]{0:T(1024)(128)(4,1)} %bitcast.101), calls=%async_computation.5 | async-start | bytes 8388608
  395.5 11.1 %slice-start.1 = ((s8[18874368]{0:T(1024)(128)(4,1)}), s8[4194304]{0:T(1024)(128)(4,1)S(1)}, s32[]{:S(2)}) async-start(s8[18874368]{0:T(1024)(128)(4,1)} %bitcast.101), calls=%async_computation.6 | async-start | bytes 8388608
  399.3 7.3 slice-start.2
  399.3 7.3 slice-start.3
  399.3 7.8 slice-start.4
  407.2 8.9 copy-start.5
  407.2 8.9 copy-start.32
  407.2 8.9 copy-start.34
  407.2 8.9 copy-start.40
  407.2 8.9 copy-start.57
  424.9 334.9 %reduce-scatter.5.cloned.1.call-start = ((), (), s32[]{:S(2)}) async-start(), calls=%async_computation.3 | async-start | bytes 9732096 | tf_op jit(solution)/shard_map/reduce_scatter | solution.py:162
  441.4 460.0 %reduce-scatter.3.cloned.1.call-start = ((), (), s32[]{:S(2)}) async-start(), calls=%async_computation.2 | async-start | bytes 9732096 | tf_op jit(solution)/shard_map/reduce_scatter | solution.py:163
  (43 other events, 152.1 us)
Sparse Core Ops, SparseCore 0:
  425.0 191.9 all-reduce.5
  623.5 136.2 reduce-scatter.4
  766.2 135.1 reduce-scatter.2
where the time goes:
time: 921 us; the launch traced here: 916 us
  waiting for transfers between devices  380 us (41%)
  matrix products  302 us (33%)
  blocking collectives  83.2 us (9%)
  local copies, waits for them, and re-layouts  72.6 us (8%)
  other arithmetic  61.1 us (7%)
  between operations  16.8 us (2%)
    reduce_scatter x1, waiting for transfers between devices, local(): lax.psum_scatter(grad_down, 'rows', scatter_dimension=0, tiled=True)  143 us
    reduce_scatter x1, waiting for transfers between devices, local(): lax.psum_scatter(grad_up_cols, 'rows', scatter_dimension=0, tiled=True)  142 us
    psum x1, waiting for transfers between devices, local(): lax.psum((grad_gain_one, grad_bias_one, grad_qkv_local, grad_wout, grad_g...  95.8 us
    dot_general x2, matrix products, forward_pass(): pre_act = jnp.dot(normed_two_low, w_up, preferred_element_type=jnp.float32)  68.6 us
    psum x1, blocking collectives, local(): query_sum = lax.psum(query_count[0].astype(jnp.float32), 'rows')  42.2 us
    psum x1, blocking collectives, local(): lax.psum((grad_gain_one, grad_bias_one, grad_qkv_local, grad_wout, grad_g...  41.1 us
    dot_general x4, matrix products, contract_rows(): lax.dot_general(left, right, (((0,), (0,)), ((), ())), preferred_element_...  39.3 us
    unnamed x150, local copies, waits for them, and re-layouts  38.4 us
  transfers between devices with their start and end apart: 3, of which 3 were waited for; matrix products, arithmetic and copies ran while one was open for 6% of the time, Pallas kernels for 0%

commit v1 on v0

v1 whole, which is shorter than its diff:
```python
from functools import partial
import math

import jax
import jax.numpy as jnp
from jax import lax
from jax.experimental import pallas as pl
from jax.experimental.pallas import tpu as pltpu
from jax.sharding import PartitionSpec as P

HEADS = 12
HEAD = 64
WINDOW = 256

epsilon = 1e-05
masked_score = -1000000000.0
root_half = math.sqrt(0.5)
root_two_pi = math.sqrt(2.0 / math.pi) * 0.5


def normalize(values, gain, bias):
    centre = jnp.mean(values, axis=-1, keepdims=True)
    centred = values - centre
    spread = jnp.mean(centred * centred, axis=-1, keepdims=True)
    inverse = lax.rsqrt(spread + epsilon)
    unit_rows = centred * inverse
    return (unit_rows * gain + bias, unit_rows, inverse)


def norm_back(grad_norm, unit_rows, inverse, gain):
    grad_unit = grad_norm * gain
    grad_mean = jnp.mean(grad_unit, axis=-1, keepdims=True)
    grad_proj = jnp.mean(grad_unit * unit_rows, axis=-1, keepdims=True)
    grad_values = inverse * (grad_unit - grad_mean - unit_rows * grad_proj)
    return (grad_values, jnp.sum(grad_norm * unit_rows, axis=0), jnp.sum(grad_norm, axis=0))


def dot(left, right, left_dim=1, right_dim=0):
    return lax.dot_general(
        left, right, (((left_dim,), (right_dim,)), ((), ())), preferred_element_type=jnp.float32
    )


def lane_masks(width):
    lanes = lax.broadcasted_iota(jnp.int32, (1, width), 1)
    return (lanes < HEAD, lanes >= HEAD)


def head_scores(query, key_rows, live, lanes):
    only = jnp.where(lanes, query, jnp.zeros_like(query)) * jnp.bfloat16(1.0 / math.sqrt(HEAD))
    return jnp.where(live, dot(only, key_rows, 1, 1), masked_score)


def attend_kernel(query_ref, key_ref, value_ref, live_ref, out_ref):
    live = live_ref[...] > 0
    query, key_rows, value_rows = query_ref[...], key_ref[...], value_ref[...]
    parts = []
    for lanes in lane_masks(2 * HEAD):
        scores = head_scores(query, key_rows, live, lanes)
        exponent = jnp.exp(scores - jnp.max(scores, axis=-1, keepdims=True))
        inverse = 1.0 / jnp.sum(exponent, axis=-1, keepdims=True)
        parts.append(dot((exponent * inverse).astype(jnp.bfloat16), value_rows))
    out_ref[...] = jnp.where(lane_masks(2 * HEAD)[0], parts[0], parts[1]).astype(jnp.bfloat16)


def attend(query_rows, packed_keys, key_live, block):
    slots, width = query_rows.shape
    keys_len = packed_keys.shape[0]
    pairs = width // (2 * HEAD)
    return pl.pallas_call(
        attend_kernel,
        grid=(pairs, slots // block),
        in_specs=[
            pl.BlockSpec((block, 2 * HEAD), lambda p, r: (r, p)),
            pl.BlockSpec((keys_len, 2 * HEAD), lambda p, r: (0, p)),
            pl.BlockSpec((keys_len, 2 * HEAD), lambda p, r: (0, pairs + p)),
            pl.BlockSpec((1, keys_len), lambda p, r: (0, 0)),
        ],
        out_specs=pl.BlockSpec((block, 2 * HEAD), lambda p, r: (r, p)),
        out_shape=jax.ShapeDtypeStruct((slots, width), jnp.bfloat16),
    )(query_rows, packed_keys, packed_keys, key_live)


def attend_back_kernel(query_ref, key_ref, value_ref, grad_ref, live_ref, dq_ref, dk_ref, dv_ref):
    live = live_ref[...] > 0
    query, key_rows, value_rows = query_ref[...], key_ref[...], value_ref[...]
    grad = grad_ref[...]
    factor = 1.0 / math.sqrt(HEAD)
    parts = []
    for lanes in lane_masks(2 * HEAD):
        scores = head_scores(query, key_rows, live, lanes)
        exponent = jnp.exp(scores - jnp.max(scores, axis=-1, keepdims=True))
        probs = exponent * (1.0 / jnp.sum(exponent, axis=-1, keepdims=True))
        grad_probs = dot(jnp.where(lanes, grad, jnp.zeros_like(grad)), value_rows, 1, 1)
        inner = jnp.sum(grad_probs * probs, axis=-1, keepdims=True)
        grad_scores = (probs * (grad_probs - inner)).astype(jnp.bfloat16)
        parts.append(
            (
                dot(grad_scores, key_rows),
                dot(grad_scores, query, 0, 0),
                dot(probs.astype(jnp.bfloat16), grad, 0, 0),
            )
        )
    first = lane_masks(2 * HEAD)[0]
    dq_ref[...] = (jnp.where(first, parts[0][0], parts[1][0]) * factor).astype(jnp.bfloat16)
    dk_ref[...] = (jnp.where(first, parts[0][1], parts[1][1]) * factor).astype(jnp.bfloat16)
    dv_ref[...] = jnp.where(first, parts[0][2], parts[1][2]).astype(jnp.bfloat16)


def attend_back(query_rows, packed_keys, grad_rows, key_live):
    width = query_rows.shape[1]
    slots = grad_rows.shape[0]
    keys_len = packed_keys.shape[0]
    pairs = width // (2 * HEAD)
    rows_spec = pl.BlockSpec((slots, 2 * HEAD), lambda p: (0, p))
    keys_spec = pl.BlockSpec((keys_len, 2 * HEAD), lambda p: (0, p))
    return pl.pallas_call(
        attend_back_kernel,
        grid=(pairs,),
        in_specs=[
            rows_spec,
            keys_spec,
            pl.BlockSpec((keys_len, 2 * HEAD), lambda p: (0, pairs + p)),
            rows_spec,
            pl.BlockSpec((1, keys_len), lambda p: (0, 0)),
        ],
        out_specs=(rows_spec, keys_spec, keys_spec),
        out_shape=(
            jax.ShapeDtypeStruct((slots, width), jnp.bfloat16),
            jax.ShapeDtypeStruct((keys_len, width), jnp.bfloat16),
            jax.ShapeDtypeStruct((keys_len, width), jnp.bfloat16),
        ),
    )(query_rows, packed_keys, packed_keys, grad_rows, key_live)


def gelu_parts(values):
    share = 0.5 * (1.0 + lax.erf(values * root_half))
    return share


def local(
    devices,
    inputs,
    context_count,
    query_count,
    row_mask,
    ln1_gain,
    ln1_bias,
    w_qkv,
    w_out,
    ln2_gain,
    ln2_bias,
    w_up,
    w_down,
    cotangent,
):
    slots, width = inputs.shape
    hidden = w_up.shape[1]
    half = hidden // 2
    me = lax.axis_index("rows")
    core = me & 1

    def bit_of(bit):
        return ((me & bit) != 0).astype(jnp.int32)

    def swap(value, bit):
        return lax.ppermute(value, "rows", [(i, i ^ bit) for i in range(devices)])

    def pick(value, axis, index):
        return lax.dynamic_index_in_dim(value, index, axis, keepdims=False)

    bits = []
    bit = 2
    while bit < devices:
        bits.append(bit)
        bit *= 2
    top = bits[-1]

    def order_of(list_of_bits, flip):
        if flip and len(list_of_bits) > 1:
            return [list_of_bits[1], list_of_bits[0]] + list_of_bits[2:]
        return list_of_bits

    context = context_count[0]
    queries = query_count[0]
    place = (jnp.arange(slots, dtype=jnp.int32) + context) & (slots - 1)
    mask_rolled = lax.dynamic_slice(jnp.concatenate([row_mask, row_mask]), (context,), (slots,))
    rows_rolled = lax.dynamic_slice(
        jnp.concatenate([inputs, inputs], axis=0), (context, 0), (slots, width)
    )
    present = (mask_rolled == 1) | (place == 0)
    row_live = present & (place < context + queries)
    key_live = (present & (place < context))[WINDOW:].astype(jnp.float32)[None, :]
    is_query = (row_live & (place >= context))[:WINDOW]
    upstream_low = lax.dynamic_slice(cotangent, (context, 0), (WINDOW, width))
    upstream = upstream_low.astype(jnp.float32) * is_query.astype(jnp.float32)[:, None]
    upstream_got = 2.0 * swap(upstream * 0.5, 1)
    upstream_both = jnp.concatenate([upstream, upstream_got], axis=0).astype(jnp.bfloat16)

    rows_wide = rows_rolled.astype(jnp.float32)
    normed, unit_one, inverse_one = normalize(rows_wide, ln1_gain, ln1_bias)
    normed_low = normed.astype(jnp.bfloat16)
    w_keys = w_qkv[:, width:]
    w_query = w_qkv[:, :width]
    packed_keys = dot(normed_low[WINDOW:], w_keys).astype(jnp.bfloat16)
    query_rows = dot(normed_low, w_query).astype(jnp.bfloat16)
    attended_q = attend(query_rows[:WINDOW], packed_keys, key_live, WINDOW)
    attended_q = jnp.where(row_live[:WINDOW, None], attended_q, jnp.bfloat16(0))
    hidden_q = rows_wide[:WINDOW] + dot(attended_q, w_out)
    _, unit_two, inverse_two = normalize(hidden_q, ln2_gain, ln2_bias)
    unit_both = jnp.concatenate([unit_two, swap(unit_two, 1)], axis=0)
    normed_two_both = (unit_both * ln2_gain + ln2_bias).astype(jnp.bfloat16)
    up_half = lax.dynamic_slice(w_up, (0, core * half), (width, half))
    down_half = lax.dynamic_slice(w_down, (core * half, 0), (half, width))
    pre_act = dot(normed_two_both, up_half)
    share = gelu_parts(pre_act)
    activated = (pre_act * share).astype(jnp.bfloat16)
    slope = share + pre_act * (root_two_pi * jnp.exp(-0.5 * pre_act * pre_act))
    grad_act = dot(upstream_both, down_half, 1, 1)
    grad_pre = (grad_act * slope).astype(jnp.bfloat16)
    grad_down = dot(activated, upstream_both, 0, 0)
    grad_up = dot(grad_pre, normed_two_both, 0, 0)

    grad_two_parts = dot(grad_pre, up_half, 1, 1)
    down_parts = dot(activated, down_half)
    grad_normed_two = grad_two_parts[:WINDOW] + swap(grad_two_parts[WINDOW:], 1)
    out_q = hidden_q + down_parts[:WINDOW] + swap(down_parts[WINDOW:], 1)

    def scatter_ff(value, flip):
        remaining = bits[:-1][::-1] + [1]
        value = value.reshape([2] * len(remaining) + [half // (2 ** len(remaining)), width])
        for bit in order_of(bits[:-1], flip):
            axis = remaining.index(bit)
            mine = bit_of(bit)
            got = swap(pick(value, axis, 1 - mine), bit)
            value = pick(value, axis, mine) + got
            remaining.remove(bit)
        pairs = [(i, i ^ top) for i in range(devices) if ((i & top) != 0) != ((i & 1) != 0)]
        value = value + lax.ppermute(value, "rows", pairs)
        other = swap(pick(value, 0, 1 - core), 1)
        return jnp.where(bit_of(top) == core, pick(value, 0, core), other)

    down_share = scatter_ff(grad_down, False)
    up_share = scatter_ff(grad_up, True)

    grad_hidden_norm, gain_two, bias_two = norm_back(
        grad_normed_two, unit_two, inverse_two, ln2_gain
    )
    grad_hidden = upstream + grad_hidden_norm
    grad_hidden_low = grad_hidden.astype(jnp.bfloat16)
    grad_wout = dot(attended_q, grad_hidden_low, 0, 0)
    grad_attended = dot(grad_hidden_low, w_out, 1, 1)
    grad_attended = jnp.where(row_live[:WINDOW, None], grad_attended, 0.0).astype(jnp.bfloat16)
    grad_query, grad_key, grad_value = attend_back(
        query_rows, packed_keys, grad_attended, key_live
    )
    grad_wq = dot(normed_low[:WINDOW], grad_query, 0, 0)
    grad_wk = dot(normed_low[WINDOW:], grad_key, 0, 0)
    grad_wv = dot(normed_low[WINDOW:], grad_value, 0, 0)
    is_odd = core == 1
    keep = [jnp.where(is_odd, grad_wk, grad_wq), jnp.where(is_odd, grad_wv, grad_wout)]
    give = [jnp.where(is_odd, grad_wq, grad_wk), jnp.where(is_odd, grad_wout, grad_wv)]

    grad_normed = jnp.concatenate(
        [
            dot(grad_query, w_query, 1, 1),
            dot(grad_key, w_keys[:, :width], 1, 1) + dot(grad_value, w_keys[:, width:], 1, 1),
        ],
        axis=0,
    )
    grad_rows, gain_one, bias_one = norm_back(grad_normed, unit_one, inverse_one, ln1_gain)
    small = jnp.concatenate(
        [
            gain_one[None],
            bias_one[None],
            gain_two[None],
            bias_two[None],
            jnp.full((4, width), queries, jnp.float32),
        ],
        axis=0,
    )
    small, keep[0] = lax.optimization_barrier((small, keep[0]))
    for bit in [1] + bits:
        small = small + swap(small, bit)
    loss_factor = math.sqrt(devices) * (slots // 4) / small[4, 0]

    def reduce_all(own, give, flip):
        value = own + swap(give, 1)
        remaining = bits[::-1]
        value = value.reshape([2] * len(remaining) + [width // (2 ** len(remaining)), width])
        order = order_of(bits, flip)
        for bit in order:
            axis = remaining.index(bit)
            mine = bit_of(bit)
            got = swap(pick(value, axis, 1 - mine), bit)
            value = pick(value, axis, mine) + got
            remaining.remove(bit)
        value = value * loss_factor
        for bit in order[::-1]:
            axis = sum(1 for b in remaining if b > bit)
            got = swap(value, bit)
            high = bit_of(bit) == 1
            value = jnp.stack([jnp.where(high, got, value), jnp.where(high, value, got)], axis=axis)
            remaining.append(bit)
        value = value.reshape(width, width)
        return (value, swap(value, 1))

    first_own, first_got = reduce_all(keep[0], give[0], False)
    second_own, second_got = reduce_all(keep[1], give[1], True)
    grad_qkv = jnp.concatenate(
        [
            jnp.where(is_odd, first_got, first_own),
            jnp.where(is_odd, first_own, first_got),
            jnp.where(is_odd, second_own, second_got),
        ],
        axis=1,
    )
    grad_out = jnp.where(is_odd, second_got, second_own)

    normed_low_c, _ = lax.optimization_barrier((query_rows, grad_up))
    context_queries = normed_low_c[WINDOW:]
    attended_c = attend(context_queries, packed_keys, key_live, WINDOW)
    attended_c = jnp.where(row_live[WINDOW:, None], attended_c, jnp.bfloat16(0))
    hidden_c = rows_wide[WINDOW:] + dot(attended_c, w_out)
    normed_two_c = normalize(hidden_c, ln2_gain, ln2_bias)[0].astype(jnp.bfloat16)
    pre_c = dot(normed_two_c, w_up)
    activated_c = (pre_c * gelu_parts(pre_c)).astype(jnp.bfloat16)
    out_c = hidden_c + dot(activated_c, w_down)

    layer_rolled = jnp.concatenate([out_q, out_c], axis=0).astype(jnp.bfloat16)
    grad_rolled = loss_factor * jnp.concatenate(
        [grad_hidden + grad_rows[:WINDOW], grad_rows[WINDOW:]], axis=0
    )

    def unroll(value):
        return lax.dynamic_slice(
            jnp.concatenate([value, value], axis=0), (slots - context, 0), (slots, width)
        )

    return (
        unroll(layer_rolled),
        unroll(grad_rolled),
        small[0] * loss_factor,
        small[1] * loss_factor,
        grad_qkv,
        grad_out,
        small[2] * loss_factor,
        small[3] * loss_factor,
        (up_share * loss_factor).T,
        down_share * loss_factor,
    )


def solution(mesh):
    placed = (
        P("rows", None),
        P("rows"),
        P("rows"),
        P("rows"),
        P(),
        P(),
        P(),
        P(),
        P(),
        P(),
        P(),
        P(),
        P("rows", None),
    )
    return jax.shard_map(
        partial(local, mesh.shape["rows"]),
        mesh=mesh,
        in_specs=placed,
        out_specs=(
            P("rows", None),
            P("rows", None),
            P(),
            P(),
            P(),
            P(),
            P(),
            P(),
            P(None, "rows"),
            P("rows", None),
        ),
        check_vma=False,
    )
```

time: 921 us -> 408 us (0.44)
  matrix products: 302 us -> 56.2 us
  waiting for transfers between devices: 380 us -> 194 us
  blocking collectives: 83.2 us -> 0 us
  local copies, waits for them, and re-layouts: 72.6 us -> 20.9 us
  Pallas kernels: 0 us -> 49.1 us
  starting transfers between devices: 0.12 us -> 32.4 us
  other arithmetic: 61.1 us -> 46.9 us
  between operations: 16.8 us -> 4.33 us
    reduce_scatter x2 -> x0, waiting for transfers between devices: 284 us -> none  [the longest x1 143 us: local(): lax.psum_scatter(grad_down, 'rows', scatter_dimension=0, tiled=True)]
    dot_general x29 -> x19, matrix products: 278 us -> 56.2 us  [dot(): lax.dot_general(left, right, (((left_dim,), (right_dim,)), ((), ())), pre...]
    ppermute x0 -> x39, waiting for transfers between devices: none -> 194 us  [the longest x37 175 us: swap(): return lax.ppermute(value, 'rows', [(i, i ^ bit) for i in range(devices)])]
    psum x1 -> x0, waiting for transfers between devices: 95.8 us -> none  [local(): lax.psum((grad_gain_one, grad_bias_one, grad_qkv_local, grad_wout, grad_g...]
    psum x2 -> x0, blocking collectives: 83.2 us -> none  [the longest x1 42.2 us: local(): query_sum = lax.psum(query_count[0].astype(jnp.float32), 'rows')]
    pallas_call x0 -> x3, Pallas kernels: none -> 49.1 us  [the longest x2 35 us: attend(): pl.pallas_call(attend_kernel, grid=(pairs, slots // block), in_specs=[pl....]
    ppermute x0 -> x39, starting transfers between devices: none -> 32.4 us  [the longest x37 29.6 us: swap(): return lax.ppermute(value, 'rows', [(i, i ^ bit) for i in range(devices)])]
    unnamed x150 -> x120, local copies, waits for them, and re-layouts: 38.4 us -> 8.33 us
  transfers between devices with their start and end apart: 3 -> 39, of which waited for: 3 -> 20; matrix products, arithmetic and copies ran while one was open for 6% -> 24% of each run, Pallas kernels for 0% -> 10%
where the time goes in v1:
time: 408 us; the launch traced here: 404 us
  waiting for transfers between devices  194 us (48%)
  matrix products  56.2 us (14%)
  Pallas kernels  49.1 us (12%)
  other arithmetic  46.9 us (11%)
  starting transfers between devices  32.4 us (8%)
  local copies, waits for them, and re-layouts  20.9 us (5%)
  between operations  4.33 us (1%)
    ppermute x37, waiting for transfers between devices, swap(): return lax.ppermute(value, 'rows', [(i, i ^ bit) for i in range(devices)])  175 us
    dot_general x19, matrix products, dot(): lax.dot_general(left, right, (((left_dim,), (right_dim,)), ((), ())), pre...  56.2 us
    pallas_call x2, Pallas kernels, attend(): pl.pallas_call(attend_kernel, grid=(pairs, slots // block), in_specs=[pl....  35 us
    ppermute x37, starting transfers between devices, swap(): return lax.ppermute(value, 'rows', [(i, i ^ bit) for i in range(devices)])  29.6 us
    ppermute x2, waiting for transfers between devices, scatter_ff(): value = value + lax.ppermute(value, 'rows', pairs)  18.7 us
    pallas_call x1, Pallas kernels, attend_back(): pl.pallas_call(attend_back_kernel, grid=(pairs,), in_specs=[rows_spec, ke...  14 us
    concatenate x2, other arithmetic, unroll(): jnp.concatenate([value, value], axis=0)  8.5 us
    unnamed x120, local copies, waits for them, and re-layouts  8.33 us
  transfers between devices with their start and end apart: 39, of which 20 were waited for; matrix products, arithmetic and copies ran while one was open for 24% of the time, Pallas kernels for 10%

profile of v1, /device:TPU:0, one launch (start us, length us, event | category | flops | bytes accessed | tf_op | source)
XLA Modules:
  0.0 403.5 jit_solution(2707505326563745808)
XLA Ops:
  7.4 3.4 convolution_convert_fusion.key_ref.value_ref
  15.5 9.7 %shard_map.204 = bf16[256,768]{1,0:T(8,128)(2,1)} custom-call(bf16[256,768]{1,0:T(8,128)(2,1)} %slice.106.query_ref, bf16[768,1536]{1,0:T(8,128)(2,1)} %convolution_convert_fusion.key_ref.value_ref, bf16[768,1536]{1,0:T(8,128)(2,1)} %convolution_convert_fusion.key_ref.value_ref, f32[1,768]{1,0:T(1,128)} %reshape.125.live_ref), custom_call_target="tpu_custom_call" | custom-call | tf_op jit(solution)/shard_map/pallas_call | solution.py:70
  33.8 3.8 multiply_convert_fusion.2
  37.7 3.6 fusion.9
  49.2 5.1 %fusion.86 = f32[1536,768]{1,0:T(8,128)} fusion(bf16[512,1536]{1,0:T(8,128)(2,1)S(1)} %fusion.6, f32[256,768]{1,0:T(8,128)} %collective-permute-done, f32[256,768]{1,0:T(8,128)} %subtract_multiply_fusion.2, f32[768]{0:T(1024)S(1)} %copy-done.46, f32[768]{0:T(1024)S(1)} %copy-done.34), kind=kOutput, calls=%fused_computation.216 | convolution fusion | flops 1209532416 | bytes 7870464 | tf_op jit(solution)/shard_map/dot_general | solution.py:39
  55.4 25.4 %shard_map.205 = bf16[768,768]{1,0:T(8,128)(2,1)} custom-call(bf16[768,768]{1,0:T(8,128)(2,1)} %slice.92.query_ref, bf16[768,1536]{1,0:T(8,128)(2,1)} %convolution_convert_fusion.key_ref.value_ref, bf16[768,1536]{1,0:T(8,128)(2,1)} %convolution_convert_fusion.key_ref.value_ref, f32[1,768]{1,0:T(1,128)} %reshape.125.live_ref), custom_call_target="tpu_custom_call" | custom-call | tf_op jit(solution)/shard_map/pallas_call | solution.py:70
  80.7 3.3 fusion.93
  87.4 13.9 %add_convert_fusion.1 = bf16[768,768]{1,0:T(8,128)(2,1)} fusion(f32[768,768]{1,0:T(8,128)} %copy-done.7, bf16[3072,768]{1,0:T(8,128)(2,1)} %param.24, bf16[768,3072]{1,0:T(8,128)(2,1)} %param.23, f32[768]{0:T(1024)} %param.22, f32[768]{0:T(1024)S(1)} %copy-done.34, f32[768]{0:T(1024)} %add_rsqrt_fusion, f32[768]{0:T(1024)} %copy-done.41), kind=kOutput, calls=%fused_computation.39 | convolution fusion | flops 7263682560 | bytes 12988416 | tf_op jit(solution)/shard_map/dot_general | solution.py:39
  101.3 3.4 dynamic-slice_bitcast_fusion.1
  104.7 3.0 collective-permute-start.29
  117.8 14.0 %shard_map.206 = (bf16[256,768]{1,0:T(8,128)(2,1)}, bf16[768,768]{1,0:T(8,128)(2,1)}, bf16[768,768]{1,0:T(8,128)(2,1)}) custom-call(bf16[1024,768]{1,0:T(8,128)(2,1)} %copy-done.10, bf16[768,1536]{1,0:T(8,128)(2,1)} %convolution_convert_fusion.key_ref.value_ref, bf16[768,1536]{1,0:T(8,128)(2,1)} %convolution_convert_fusion.key_ref.value_ref, ...), custom_call_target="tpu_custom_call" | custom-call | tf_op jit(solution)/shard_map/pallas_call | solution.py:117
  131.8 2.8 fusion.39
  134.8 2.9 broadcast_select_fusion.2
  151.2 2.8 select_add_fusion
  161.8 23.4 %collective-permute-done.6 = f32[8,768]{1,0:T(8,128)S(1)} collective-permute-done((f32[8,768]{1,0:T(8,128)S(1)}, f32[8,768]{1,0:T(8,128)S(1)}, u32[]{:S(2)}, u32[]{:S(2)}) %collective-permute-start.6) | collective-permute-done | bytes 24608 | tf_op jit(solution)/shard_map/ppermute | solution.py:167
  203.2 48.9 %collective-permute-done.21 = f32[2,2,48,768]{3,2,1,0:T(8,128)S(1)} collective-permute-done((f32[2,2,48,768]{3,2,1,0:T(8,128)S(1)}, f32[2,2,48,768]{3,2,1,0:T(8,128)S(1)}, u32[]{:S(2)}, u32[]{:S(2)}) %collective-permute-start.21) | collective-permute-done | bytes 589856 | tf_op jit(solution)/shard_map/ppermute | solution.py:167
  254.4 8.8 %collective-permute-done.22 = f32[2,48,768]{2,1,0:T(8,128)S(1)} collective-permute-done((f32[2,48,768]{2,1,0:T(8,128)S(1)}, f32[2,48,768]{2,1,0:T(8,128)S(1)}, u32[]{:S(2)}, u32[]{:S(2)}) %collective-permute-start.22) | collective-permute-done | bytes 294944 | tf_op jit(solution)/shard_map/ppermute | solution.py:167
  266.9 4.0 collective-permute-start.13
  270.9 7.0 %collective-permute-done.23 = f32[48,768]{1,0:T(8,128)S(1)} collective-permute-done((f32[48,768]{1,0:T(8,128)S(1)}, f32[48,768]{1,0:T(8,128)S(1)}, u32[]{:S(2)}, u32[]{:S(2)}) %collective-permute-start.23) | collective-permute-done | bytes 147488 | tf_op jit(solution)/shard_map/ppermute | solution.py:167
  278.0 4.6 %collective-permute-done.13 = f32[48,768]{1,0:T(8,128)S(1)} collective-permute-done((f32[48,768]{1,0:T(8,128)S(1)}, f32[48,768]{1,0:T(8,128)S(1)}, u32[]{:S(2)}, u32[]{:S(2)}) %collective-permute-start.13) | collective-permute-done | bytes 147488 | tf_op jit(solution)/shard_map/ppermute | solution.py:167
  285.4 3.5 collective-permute-done.14
  289.0 6.2 %collective-permute-done.25 = f32[2,48,768]{2,1,0:T(8,128)S(1)} collective-permute-done((f32[2,48,768]{2,1,0:T(8,128)S(1)}, f32[2,48,768]{2,1,0:T(8,128)S(1)}, u32[]{:S(2)}, u32[]{:S(2)}) %collective-permute-start.25) | collective-permute-done | bytes 294944 | tf_op jit(solution)/shard_map/ppermute | solution.py:167
  295.4 3.9 collective-permute-done.15
  302.1 4.2 %collective-permute-done.26 = f32[2,2,48,768]{3,2,1,0:T(8,128)S(1)} collective-permute-done((f32[2,2,48,768]{3,2,1,0:T(8,128)S(1)}, f32[2,2,48,768]{3,2,1,0:T(8,128)S(1)}, u32[]{:S(2)}, u32[]{:S(2)}) %collective-permute-start.26) | collective-permute-done | bytes 589856 | tf_op jit(solution)/shard_map/ppermute | solution.py:167
  306.6 9.1 %collective-permute-done.16 = f32[2,2,48,768]{3,2,0,1:T(8,128)S(1)} collective-permute-done((f32[2,2,48,768]{3,2,0,1:T(8,128)S(1)}, f32[2,2,48,768]{3,2,0,1:T(8,128)S(1)}, u32[]{:S(2)}, u32[]{:S(2)}) %collective-permute-start.16) | collective-permute-done | bytes 589856 | tf_op jit(solution)/shard_map/ppermute | solution.py:167
  316.3 24.7 %collective-permute-done.35 = f32[2,2,96,768]{3,2,1,0:T(8,128)S(1)} collective-permute-done((f32[2,2,96,768]{3,2,1,0:T(8,128)S(1)}, f32[2,2,96,768]{3,2,1,0:T(8,128)S(1)}, u32[]{:S(2)}, u32[]{:S(2)}) %collective-permute-start.35) | collective-permute-done | bytes 1179680 | tf_op jit(solution)/shard_map/ppermute | solution.py:167
  341.3 21.9 %collective-permute-done.27 = f32[2,2,2,48,768]{4,3,2,1,0:T(8,128)S(1)} collective-permute-done((f32[2,2,2,48,768]{4,3,2,1,0:T(8,128)S(1)}, f32[2,2,2,48,768]{4,3,2,1,0:T(8,128)S(1)}, u32[]{:S(2)}, u32[]{:S(2)}) %collective-permute-start.27) | collective-permute-done | bytes 1179680 | tf_op jit(solution)/shard_map/ppermute | solution.py:167
  367.8 5.3 %fusion.17 = bf16[1024,768]{1,0:T(8,128)(2,1)} fusion(s32[]{:T(128)S(6)} %select_n.226, bf16[256,768]{1,0:T(8,128)(2,1)S(1)} %fusion.45, bf16[768,768]{1,0:T(8,128)(2,1)S(1)} %copy-done.28), kind=kLoop, calls=%fused_computation.55 | loop fusion | flops 6291456 | bytes 3145732 | tf_op jit(solution)/shard_map/concatenate | solution.py:337
  373.4 15.7 %collective-permute-done.32 = f32[2,96,768]{2,1,0:T(8,128)S(1)} collective-permute-done((f32[2,96,768]{2,1,0:T(8,128)S(1)}, f32[2,96,768]{2,1,0:T(8,128)S(1)}, u32[]{:S(2)}, u32[]{:S(2)}) %collective-permute-start.32) | collective-permute-done | bytes 589856 | tf_op jit(solution)/shard_map/ppermute | solution.py:239
  389.4 3.2 fusion.5
  392.6 2.9 collective-permute-done.37
  400.1 3.2 pad_maximum_fusion
  (303 shorter events, 101.3 us)
Async XLA Ops:
  32.6 10.3 %collective-permute-start.2 = (f32[256,768]{1,0:T(8,128)}, f32[256,768]{1,0:T(8,128)}, u32[]{:S(2)}, u32[]{:S(2)}) collective-permute-start(f32[256,768]{1,0:T(8,128)} %get-tuple-element.54), channel_id=1, source_target_pairs={{0,1},{1,0},{2,3},{3,2},{4,5},{5,4},{6,7},{7,6},{8,9},{9,8},{10,11... | collective-permute-start | bytes 2359304 | tf_op jit(solution)/shard_map/ppermute | solution.py:167
  42.3 144.7 %collective-permute-start.1 = (f32[256,768]{1,0:T(8,128)}, f32[256,768]{1,0:T(8,128)}, u32[]{:S(2)}, u32[]{:S(2)}) collective-permute-start(f32[256,768]{1,0:T(8,128)} %slice.109), channel_id=1, source_target_pairs={{0,1},{1,0},{2,3},{3,2},{4,5},{5,4},{6,7},{7,6},{8,9},{9,8},{10,11... | collective-permute-start | bytes 2359304 | tf_op jit(solution)/shard_map/ppermute | solution.py:167
  87.4 24.6 %collective-permute-start.3 = (f32[256,768]{1,0:T(8,128)}, f32[256,768]{1,0:T(8,128)}, u32[]{:S(2)}, u32[]{:S(2)}) collective-permute-start(f32[256,768]{1,0:T(8,128)} %slice.112), channel_id=1, source_target_pairs={{0,1},{1,0},{2,3},{3,2},{4,5},{5,4},{6,7},{7,6},{8,9},{9,8},{10,11... | collective-permute-start | bytes 2359304 | tf_op jit(solution)/shard_map/ppermute | solution.py:167
  104.7 94.8 %collective-permute-start.29 = (f32[2,2,2,96,768]{4,3,2,1,0:T(8,128)}, f32[2,2,2,96,768]{4,3,2,1,0:T(8,128)}, u32[]{:S(2)}, u32[]{:S(2)}) collective-permute-start(f32[2,2,2,96,768]{4,3,2,1,0:T(8,128)} %dynamic-slice_bitcast_fusion.1), channel_id=1, source_target_pairs={{0,4},{1,5},{2,6},{3,7},{4,0},{5,1},{6,2},{7,3},{8,12},{9,13},{10,... | collective-permute-start | bytes 7077896 | tf_op jit(solution)/shard_map/ppermute | solution.py:167
  138.0 13.2 %collective-permute-start.19 = (f32[768,768]{1,0:T(8,128)}, f32[768,768]{1,0:T(8,128)}, u32[]{:S(2)}, u32[]{:S(2)}) collective-permute-start(f32[768,768]{1,0:T(8,128)} %get-tuple-element.77), channel_id=1, source_target_pairs={{0,1},{1,0},{2,3},{3,2},{4,5},{5,4},{6,7},{7,6},{8,9},{9,8},{10,11... | collective-permute-start | bytes 7077896 | tf_op jit(solution)/shard_map/ppermute | solution.py:167
  142.4 14.1 %collective-permute-start.9 = (f32[768,768]{1,0:T(8,128)}, f32[768,768]{1,0:T(8,128)}, u32[]{:S(2)}, u32[]{:S(2)}) collective-permute-start(f32[768,768]{1,0:T(8,128)} %get-tuple-element.43), channel_id=1, source_target_pairs={{0,1},{1,0},{2,3},{3,2},{4,5},{5,4},{6,7},{7,6},{8,9},{9,8},{10,11... | collective-permute-start | bytes 7077896 | tf_op jit(solution)/shard_map/ppermute | solution.py:167
  154.3 42.6 %collective-permute-start.20 = (f32[2,2,2,48,768]{4,3,1,0,2:T(8,128)S(1)}, f32[2,2,2,48,768]{4,3,1,0,2:T(8,128)S(1)}, u32[]{:S(2)}, u32[]{:S(2)}) collective-permute-start(f32[2,2,2,48,768]{4,3,1,0,2:T(8,128)S(1)} %bitcast.169), channel_id=1, source_target_pairs={{0,4},{1,5},{2,6},{3,7},{4,0},{5,1},{6,2},{7,3},{8,12},{9,13},{10,... | collective-permute-start | bytes 3538952 | tf_op jit(solution)/shard_map/ppermute | solution.py:167
  154.8 30.5 %collective-permute-start.6 = (f32[8,768]{1,0:T(8,128)S(1)}, f32[8,768]{1,0:T(8,128)S(1)}, u32[]{:S(2)}, u32[]{:S(2)}) collective-permute-start(f32[8,768]{1,0:T(8,128)S(1)} %add.293), channel_id=1, source_target_pairs={{0,4},{1,5},{2,6},{3,7},{4,0},{5,1},{6,2},{7,3},{8,12},{9,13},{10,... | collective-permute-start | bytes 73736 | tf_op jit(solution)/shard_map/ppermute | solution.py:167
  158.7 38.7 %collective-permute-start.10 = (f32[2,2,2,48,768]{4,3,1,0,2:T(8,128)S(1)}, f32[2,2,2,48,768]{4,3,1,0,2:T(8,128)S(1)}, u32[]{:S(2)}, u32[]{:S(2)}) collective-permute-start(f32[2,2,2,48,768]{4,3,1,0,2:T(8,128)S(1)} %bitcast.170), channel_id=1, source_target_pairs={{0,2},{1,3},{2,0},{3,1},{4,6},{5,7},{6,4},{7,5},{8,10},{9,11},{10,... | collective-permute-start | bytes 3538952 | tf_op jit(solution)/shard_map/ppermute | solution.py:167
  185.3 114.3 %collective-permute-start.34 = (f32[2,2,2,96,768]{4,3,2,1,0:T(8,128)S(1)}, f32[2,2,2,96,768]{4,3,2,1,0:T(8,128)S(1)}, u32[]{:S(2)}, u32[]{:S(2)}) collective-permute-start(f32[2,2,2,96,768]{4,3,2,1,0:T(8,128)S(1)} %copy-done.17), channel_id=1, source_target_pairs={{0,2},{1,3},{2,0},{3,1},{4,6},{5,7},{6,4},{7,5},{8,10},{9,11},{10,... | collective-permute-start | bytes 7077896 | tf_op jit(solution)/shard_map/ppermute | solution.py:167
  197.1 54.9 %collective-permute-start.21 = (f32[2,2,48,768]{3,2,1,0:T(8,128)S(1)}, f32[2,2,48,768]{3,2,1,0:T(8,128)S(1)}, u32[]{:S(2)}, u32[]{:S(2)}) collective-permute-start(f32[2,2,48,768]{3,2,1,0:T(8,128)S(1)} %dynamic-slice_bitcast_fusion.6), channel_id=1, source_target_pairs={{0,2},{1,3},{2,0},{3,1},{4,6},{5,7},{6,4},{7,5},{8,10},{9,11},{10,... | collective-permute-start | bytes 1769480 | tf_op jit(solution)/shard_map/ppermute | solution.py:167
  197.7 56.3 %collective-permute-start.11 = (f32[2,2,48,768]{3,2,1,0:T(8,128)S(1)}, f32[2,2,48,768]{3,2,1,0:T(8,128)S(1)}, u32[]{:S(2)}, u32[]{:S(2)}) collective-permute-start(f32[2,2,48,768]{3,2,1,0:T(8,128)S(1)} %dynamic-slice_bitcast_fusion.7), channel_id=1, source_target_pairs={{0,4},{1,5},{2,6},{3,7},{4,0},{5,1},{6,2},{7,3},{8,12},{9,13},{10,... | collective-permute-start | bytes 1769480 | tf_op jit(solution)/shard_map/ppermute | solution.py:167
  201.6 114.4 %collective-permute-start.30 = (f32[2,2,96,768]{3,2,1,0:T(8,128)S(1)}, f32[2,2,96,768]{3,2,1,0:T(8,128)S(1)}, u32[]{:S(2)}, u32[]{:S(2)}) collective-permute-start(f32[2,2,96,768]{3,2,1,0:T(8,128)S(1)} %dynamic-slice_bitcast_fusion.3), channel_id=1, source_target_pairs={{0,2},{1,3},{2,0},{3,1},{4,6},{5,7},{6,4},{7,5},{8,10},{9,11},{10,... | collective-permute-start | bytes 3538952 | tf_op jit(solution)/shard_map/ppermute | solution.py:167
  252.1 11.0 %collective-permute-start.22 = (f32[2,48,768]{2,1,0:T(8,128)S(1)}, f32[2,48,768]{2,1,0:T(8,128)S(1)}, u32[]{:S(2)}, u32[]{:S(2)}) collective-permute-start(f32[2,48,768]{2,1,0:T(8,128)S(1)} %dynamic-slice_bitcast_fusion.10), channel_id=1, source_target_pairs={{0,8},{1,9},{2,10},{3,11},{4,12},{5,13},{6,14},{7,15},{8,0},{9,1},... | collective-permute-start | bytes 884744 | tf_op jit(solution)/shard_map/ppermute | solution.py:167
  254.1 12.7 %collective-permute-start.12 = (f32[2,48,768]{2,1,0:T(8,128)S(1)}, f32[2,48,768]{2,1,0:T(8,128)S(1)}, u32[]{:S(2)}, u32[]{:S(2)}) collective-permute-start(f32[2,48,768]{2,1,0:T(8,128)S(1)} %dynamic-slice_bitcast_fusion.11), channel_id=1, source_target_pairs={{0,8},{1,9},{2,10},{3,11},{4,12},{5,13},{6,14},{7,15},{8,0},{9,1},... | collective-permute-start | bytes 884744 | tf_op jit(solution)/shard_map/ppermute | solution.py:167
  263.2 14.7 %collective-permute-start.23 = (f32[48,768]{1,0:T(8,128)S(1)}, f32[48,768]{1,0:T(8,128)S(1)}, u32[]{:S(2)}, u32[]{:S(2)}) collective-permute-start(f32[48,768]{1,0:T(8,128)S(1)} %dynamic-slice_bitcast_fusion.12), channel_id=1, source_target_pairs={{0,16},{1,17},{2,18},{3,19},{4,20},{5,21},{6,22},{7,23},{8,24},{9,... | collective-permute-start | bytes 442376 | tf_op jit(solution)/shard_map/ppermute | solution.py:167
  266.9 15.7 %collective-permute-start.13 = (f32[48,768]{1,0:T(8,128)S(1)}, f32[48,768]{1,0:T(8,128)S(1)}, u32[]{:S(2)}, u32[]{:S(2)}) collective-permute-start(f32[48,768]{1,0:T(8,128)S(1)} %dynamic-slice_bitcast_fusion.13), channel_id=1, source_target_pairs={{0,16},{1,17},{2,18},{3,19},{4,20},{5,21},{6,22},{7,23},{8,24},{9,... | collective-permute-start | bytes 442376 | tf_op jit(solution)/shard_map/ppermute | solution.py:167
  277.9 7.3 %collective-permute-start.24 = (f32[48,768]{1,0:T(8,128)S(1)}, f32[48,768]{1,0:T(8,128)S(1)}, u32[]{:S(2)}, u32[]{:S(2)}) collective-permute-start(f32[48,768]{1,0:T(8,128)S(1)} %fusion.58), channel_id=1, source_target_pairs={{0,16},{1,17},{2,18},{3,19},{4,20},{5,21},{6,22},{7,23},{8,24},{9,... | collective-permute-start | bytes 442376 | tf_op jit(solution)/shard_map/ppermute | solution.py:167
  285.3 9.9 %collective-permute-start.25 = (f32[2,48,768]{2,1,0:T(8,128)S(1)}, f32[2,48,768]{2,1,0:T(8,128)S(1)}, u32[]{:S(2)}, u32[]{:S(2)}) collective-permute-start(f32[2,48,768]{2,1,0:T(8,128)S(1)} %pad_maximum_fusion.12), channel_id=1, source_target_pairs={{0,8},{1,9},{2,10},{3,11},{4,12},{5,13},{6,14},{7,15},{8,0},{9,1},... | collective-permute-start | bytes 884744 | tf_op jit(solution)/shard_map/ppermute | solution.py:167
  289.0 10.4 %collective-permute-start.15 = (f32[2,48,768]{2,1,0:T(8,128)S(1)}, f32[2,48,768]{2,1,0:T(8,128)S(1)}, u32[]{:S(2)}, u32[]{:S(2)}) collective-permute-start(f32[2,48,768]{2,1,0:T(8,128)S(1)} %pad_maximum_fusion.11), channel_id=1, source_target_pairs={{0,8},{1,9},{2,10},{3,11},{4,12},{5,13},{6,14},{7,15},{8,0},{9,1},... | collective-permute-start | bytes 884744 | tf_op jit(solution)/shard_map/ppermute | solution.py:167
  295.3 11.0 %collective-permute-start.26 = (f32[2,2,48,768]{3,2,1,0:T(8,128)S(1)}, f32[2,2,48,768]{3,2,1,0:T(8,128)S(1)}, u32[]{:S(2)}, u32[]{:S(2)}) collective-permute-start(f32[2,2,48,768]{3,2,1,0:T(8,128)S(1)} %pad_maximum_fusion.8), channel_id=1, source_target_pairs={{0,2},{1,3},{2,0},{3,1},{4,6},{5,7},{6,4},{7,5},{8,10},{9,11},{10,... | collective-permute-start | bytes 1769480 | tf_op jit(solution)/shard_map/ppermute | solution.py:167
  299.5 16.3 %collective-permute-start.16 = (f32[2,2,48,768]{3,2,0,1:T(8,128)S(1)}, f32[2,2,48,768]{3,2,0,1:T(8,128)S(1)}, u32[]{:S(2)}, u32[]{:S(2)}) collective-permute-start(f32[2,2,48,768]{3,2,0,1:T(8,128)S(1)} %pad_maximum_fusion.7), channel_id=1, source_target_pairs={{0,4},{1,5},{2,6},{3,7},{4,0},{5,1},{6,2},{7,3},{8,12},{9,13},{10,... | collective-permute-start | bytes 1769480 | tf_op jit(solution)/shard_map/ppermute | solution.py:167
  300.0 41.0 %collective-permute-start.35 = (f32[2,2,96,768]{3,2,1,0:T(8,128)S(1)}, f32[2,2,96,768]{3,2,1,0:T(8,128)S(1)}, u32[]{:S(2)}, u32[]{:S(2)}) collective-permute-start(f32[2,2,96,768]{3,2,1,0:T(8,128)S(1)} %dynamic-slice_bitcast_fusion.2), channel_id=1, source_target_pairs={{0,4},{1,5},{2,6},{3,7},{4,0},{5,1},{6,2},{7,3},{8,12},{9,13},{10,... | collective-permute-start | bytes 3538952 | tf_op jit(solution)/shard_map/ppermute | solution.py:167
  306.5 56.7 %collective-permute-start.27 = (f32[2,2,2,48,768]{4,3,2,1,0:T(8,128)S(1)}, f32[2,2,2,48,768]{4,3,2,1,0:T(8,128)S(1)}, u32[]{:S(2)}, u32[]{:S(2)}) collective-permute-start(f32[2,2,2,48,768]{4,3,2,1,0:T(8,128)S(1)} %pad_maximum_fusion.5), channel_id=1, source_target_pairs={{0,4},{1,5},{2,6},{3,7},{4,0},{5,1},{6,2},{7,3},{8,12},{9,13},{10,... | collective-permute-start | bytes 3538952 | tf_op jit(solution)/shard_map/ppermute | solution.py:167
  315.9 47.8 %collective-permute-start.17 = (f32[2,2,2,48,768]{4,3,0,1,2:T(8,128)S(1)}, f32[2,2,2,48,768]{4,3,0,1,2:T(8,128)S(1)}, u32[]{:S(2)}, u32[]{:S(2)}) collective-permute-start(f32[2,2,2,48,768]{4,3,0,1,2:T(8,128)S(1)} %pad_maximum_fusion.4), channel_id=1, source_target_pairs={{0,2},{1,3},{2,0},{3,1},{4,6},{5,7},{6,4},{7,5},{8,10},{9,11},{10,... | collective-permute-start | bytes 3538952 | tf_op jit(solution)/shard_map/ppermute | solution.py:167
  316.2 48.6 %collective-permute-start.31 = (f32[2,96,768]{2,1,0:T(8,128)S(1)}, f32[2,96,768]{2,1,0:T(8,128)S(1)}, u32[]{:S(2)}, u32[]{:S(2)}) collective-permute-start(f32[2,96,768]{2,1,0:T(8,128)S(1)} %dynamic-slice_bitcast_fusion.5), channel_id=1, source_target_pairs={{0,8},{1,9},{2,10},{3,11},{4,12},{5,13},{6,14},{7,15},{8,0},{9,1},... | collective-permute-start | bytes 1769480 | tf_op jit(solution)/shard_map/ppermute | solution.py:167
  341.2 25.0 %collective-permute-start.36 = (f32[2,96,768]{2,1,0:T(8,128)S(1)}, f32[2,96,768]{2,1,0:T(8,128)S(1)}, u32[]{:S(2)}, u32[]{:S(2)}) collective-permute-start(f32[2,96,768]{2,1,0:T(8,128)S(1)} %dynamic-slice_bitcast_fusion.4), channel_id=1, source_target_pairs={{0,8},{1,9},{2,10},{3,11},{4,12},{5,13},{6,14},{7,15},{8,0},{9,1},... | collective-permute-start | bytes 1769480 | tf_op jit(solution)/shard_map/ppermute | solution.py:167
  363.6 34.4 %collective-permute-start.28 = (f32[768,768]{1,0:T(8,128)S(1)}, f32[768,768]{1,0:T(8,128)S(1)}, u32[]{:S(2)}, u32[]{:S(2)}) collective-permute-start(f32[768,768]{1,0:T(8,128)S(1)} %bitcast.167), channel_id=1, source_target_pairs={{0,1},{1,0},{2,3},{3,2},{4,5},{5,4},{6,7},{7,6},{8,9},{9,8},{10,11... | collective-permute-start | bytes 7077896 | tf_op jit(solution)/shard_map/ppermute | solution.py:167
  364.2 35.5 %collective-permute-start.18 = (f32[768,768]{1,0:T(8,128)S(1)}, f32[768,768]{1,0:T(8,128)S(1)}, u32[]{:S(2)}, u32[]{:S(2)}) collective-permute-start(f32[768,768]{1,0:T(8,128)S(1)} %bitcast.168), channel_id=1, source_target_pairs={{0,1},{1,0},{2,3},{3,2},{4,5},{5,4},{6,7},{7,6},{8,9},{9,8},{10,11... | collective-permute-start | bytes 7077896 | tf_op jit(solution)/shard_map/ppermute | solution.py:167
  364.9 24.3 %collective-permute-start.32 = (f32[2,96,768]{2,1,0:T(8,128)S(1)}, f32[2,96,768]{2,1,0:T(8,128)S(1)}, u32[]{:S(2)}, u32[]{:S(2)}) collective-permute-start(f32[2,96,768]{2,1,0:T(8,128)S(1)} %bitcast_add_fusion.7), channel_id=1, source_target_pairs={{1,17},{3,19},{5,21},{7,23},{9,25},{11,27},{13,29},{15,31},{16,0},... | collective-permute-start | bytes 1769480 | tf_op jit(solution)/shard_map/ppermute | solution.py:239
  366.3 29.2 %collective-permute-start.37 = (f32[2,96,768]{2,1,0:T(8,128)S(1)}, f32[2,96,768]{2,1,0:T(8,128)S(1)}, u32[]{:S(2)}, u32[]{:S(2)}) collective-permute-start(f32[2,96,768]{2,1,0:T(8,128)S(1)} %bitcast_add_fusion.6), channel_id=1, source_target_pairs={{1,17},{3,19},{5,21},{7,23},{9,25},{11,27},{13,29},{15,31},{16,0},... | collective-permute-start | bytes 1769480 | tf_op jit(solution)/shard_map/ppermute | solution.py:239
  389.3 7.0 %collective-permute-start.33 = (f32[96,768]{1,0:T(8,128)S(1)}, f32[96,768]{1,0:T(8,128)S(1)}, u32[]{:S(2)}, u32[]{:S(2)}) collective-permute-start(f32[96,768]{1,0:T(8,128)S(1)} %dynamic-slice_bitcast_fusion.9), channel_id=1, source_target_pairs={{0,1},{1,0},{2,3},{3,2},{4,5},{5,4},{6,7},{7,6},{8,9},{9,8},{10,11... | collective-permute-start | bytes 884744 | tf_op jit(solution)/shard_map/ppermute | solution.py:167
  (67 other events, 423.5 us)
